TPU v7x, 256 devices: a whole 4x4x8 slice. The times are simulated.
256 devices in a mesh: dp: 2 (over core), tensor: 8 (over z), expert: 16 (over y, x).
Axes of the slice: x: 4, y: 4, z: 8, core: 2. Of those that a mesh axis runs over, the one named last changes fastest.
Arguments:
- attn_heads: bfloat16 [32, 64, 4096], P(('dp', 'expert'), None, 'tensor'), may hold values from -6 to 6
- out_proj: bfloat16 [4096, 4096], P('tensor'), may hold values from -0.09375 to 0.09375
- residual: bfloat16 [32, 64, 4096], P(('dp', 'expert'), 'tensor'), may hold values from -6 to 6
- norm_gain: float32 [4096], replicated, may hold values from 0.25 to 1.75
- expert_ids: int32 [32, 64, 8], P(('dp', 'expert'), 'tensor'), may hold values from 0 to 15, all different within a row; in each aligned block of 8 rows (0 to 7, 8 to 15, ..., all dimensions but the last counted through in order) at most 6 rows name the same one
- weight_codes: int32 [32, 64, 8], P(('dp', 'expert'), 'tensor'), may hold values from 1 to 16
- w_gate: bfloat16 [16, 1536, 4096], P('expert', 'tensor'), may hold values from -0.09375 to 0.09375
- w_up: bfloat16 [16, 1536, 4096], P('expert', 'tensor'), may hold values from -0.09375 to 0.09375
- w_down: bfloat16 [16, 1536, 4096], P('expert', 'tensor'), may hold values from -0.625 to 0.625
Outputs:
- layer_out: bfloat16 [32, 64, 4096], P(('dp', 'expert'), 'tensor')
Inputs may be any that keep to these rules, and one draw needn't show every extreme that they name: `expert_ids`: each token names 8 different experts. Among the 8 consecutive tokens of one device (aligned blocks of the flattened first two dimensions) no expert is named by more than 6 rows, and every draw has an expert named exactly 6 times in some device's rows.
All inputs are finite; a program needn't handle non-finite values.
Results may differ from a plain program's by a relative error of at most 0.022.
Values may be sent and summed in bfloat16 or wider, within the bound.
No kernel may reach another device: no remote copies, remote signals or barrier semaphores. Data moves between devices by JAX's collectives and lax.ppermute only.
A program may use at most 128 MiB of HBM per device.

v0:
```python
import jax
import jax.numpy as jnp
from jax import lax
from jax.sharding import PartitionSpec as P

EXPERTS = 16
TOP = 8
CAP = 6


def normalize(hidden, norm_gain):
    mean_square = jnp.mean(hidden * hidden, axis=-1, keepdims=True)
    return (hidden * lax.rsqrt(mean_square + 1e-06) * norm_gain).astype(jnp.bfloat16)


def place_rows(route_ids, per_device):
    flat_rows = route_ids.reshape(-1)
    one_hot = (flat_rows[:, None] == jnp.arange(EXPERTS, dtype=jnp.int32)[None, :]).astype(
        jnp.int32
    )
    position = jnp.sum((jnp.cumsum(one_hot, axis=0) - one_hot) * one_hot, axis=1)
    owner_dev = flat_rows // per_device
    local_expert = flat_rows % per_device
    slot_index = owner_dev * (CAP * per_device) + position * per_device + local_expert
    return slot_index.reshape(route_ids.shape)


def build_outgoing(normed, slot_index, slot_count):
    placement = jnp.any(
        slot_index[None, :, :] == jnp.arange(slot_count, dtype=jnp.int32)[:, None, None], axis=2
    )
    return jnp.dot(
        placement.astype(jnp.bfloat16), normed, preferred_element_type=jnp.float32
    ).astype(jnp.bfloat16)


def on_device(
    attn_heads, out_proj, residual, norm_gain, expert_ids, weight_codes, w_gate, w_up, w_down
):
    tensor_count = lax.axis_size("tensor")
    expert_count = lax.axis_size("expert")
    per_device = w_gate.shape[0]
    head_rows = attn_heads[0]
    own_residual = residual[0]
    own_ids = expert_ids[0]
    own_codes = weight_codes[0]
    tok_own = own_residual.shape[0]
    model_width = own_residual.shape[1]
    slot_count = expert_count * CAP * per_device
    attn_sum = lax.psum_scatter(
        jnp.dot(head_rows, out_proj, preferred_element_type=jnp.float32).astype(jnp.bfloat16),
        "tensor",
        scatter_dimension=0,
        tiled=True,
    ).astype(jnp.float32)
    hidden = own_residual.astype(jnp.float32) + attn_sum
    normed = normalize(hidden, norm_gain)
    slot_index = place_rows(own_ids, per_device)
    outgoing = build_outgoing(normed, slot_index, slot_count).reshape(
        expert_count, CAP * per_device, model_width
    )
    arrived = lax.all_to_all(outgoing, "expert", split_axis=0, concat_axis=0, tiled=True)
    arrived = arrived.reshape(expert_count * CAP, per_device, model_width)
    portion = lax.all_gather(arrived, "tensor", axis=0, tiled=True)
    gate_value = jnp.einsum("red,efd->ref", portion, w_gate, preferred_element_type=jnp.float32)
    up_value = jnp.einsum("red,efd->ref", portion, w_up, preferred_element_type=jnp.float32)
    activated = (jax.nn.silu(gate_value) * up_value).astype(jnp.bfloat16)
    partial_out = jnp.einsum("ref,efd->red", activated, w_down, preferred_element_type=jnp.float32)
    partial_out = partial_out.astype(jnp.bfloat16).reshape(
        tensor_count * expert_count, CAP * per_device, model_width
    )
    received = lax.all_to_all(
        partial_out, ("tensor", "expert"), split_axis=0, concat_axis=0, tiled=True
    )
    received = received.reshape(tensor_count, slot_count, model_width)
    returned_flat = jnp.sum(received, axis=0, dtype=jnp.float32).astype(jnp.bfloat16)
    picked = jnp.take(returned_flat, slot_index.reshape(-1), axis=0).reshape(
        tok_own, TOP, model_width
    )
    code_values = own_codes.astype(jnp.float32)
    mixing = code_values / jnp.sum(code_values, axis=-1, keepdims=True)
    expert_mix = jnp.sum(mixing[:, :, None] * picked.astype(jnp.float32), axis=1)
    layer_out = (hidden + expert_mix).astype(jnp.bfloat16)
    return layer_out[None]


def solution(mesh):
    return jax.shard_map(
        on_device,
        mesh=mesh,
        in_specs=(
            P(("dp", "expert"), None, "tensor"),
            P("tensor", None),
            P(("dp", "expert"), "tensor", None),
            P(),
            P(("dp", "expert"), "tensor", None),
            P(("dp", "expert"), "tensor", None),
            P("expert", "tensor", None),
            P("expert", "tensor", None),
            P("expert", "tensor", None),
        ),
        out_specs=P(("dp", "expert"), "tensor", None),
        check_vma=False,
    )
```

profile of v0, /device:TPU:6, one launch (start us, length us, event | category | flops | bytes accessed | tf_op | source)
XLA Modules:
  0.0 396.0 jit_solution(4905630625477676545)
XLA Ops:
  6.5 0.0 copy-start
  6.5 0.0 copy-start.4
  6.5 0.0 copy-start.2
  6.5 0.0 copy-start.5
  6.5 0.0 reduce-scatter.2.cloned.1.call-start
  6.6 4.0 %convolution_convert_fusion.2 = bf16[64,4096]{1,0:T(8,128)(2,1)} fusion(bf16[512,4096]{1,0:T(8,128)(2,1)} %param.10, bf16[1,64,512]{2,1,0:T(8,128)(2,1)} %param.9), kind=kOutput, calls=%fused_computation.8 | convolution fusion | flops 268697600 | bytes 4784128 | tf_op jit(solution)/shard_map/dot_general | solution.py:51
  10.6 0.0 reduce-scatter.2.cloned.1.call-update
  10.6 0.0 all-gather.2.cloned.1.call-start
  10.6 0.0 copy-done.4
  10.6 0.1 reshape_squeeze.3
  10.7 0.1 fusion.48
  10.8 0.1 reduce_window_sum.11
  10.9 0.2 select_reduce_fusion
  11.1 0.1 reduce_sum.57
  11.2 0.1 fusion.49
  11.3 39.6 %reduce-scatter.2.cloned.1.call-done = bf16[8,4096]{1,0:T(8,128)(2,1)} async-done(((bf16[64,4096]{1,0:T(8,128)(2,1)}), bf16[8,4096]{1,0:T(8,128)(2,1)}) %reduce-scatter.2.cloned.1.call-update) | async-done | bytes 65552 | tf_op jit(solution)/shard_map/reduce_scatter | solution.py:50
  50.9 0.0 copy-done.2
  50.9 1.0 multiply_reduce_fusion.1
  51.9 0.0 copy-done.5
  51.9 1.3 convolution_convert_fusion.1
  53.1 0.3 reshape.115
  53.4 17.6 %all_to_all.10 = bf16[16,6,4096]{2,1,0:T(8,128)(2,1)} all-to-all(bf16[16,6,4096]{2,1,0:T(8,128)(2,1)S(1)} %reshape.115), channel_id=1, replica_groups=mesh['dp'=2,'tensor'=8,'expert'=16] {'expert'}, dimensions={0} | all-to-all | bytes 1572864 | tf_op jit(solution)/shard_map/all_to_all | solution.py:62
  71.0 2.2 reshape.116
  73.2 0.0 all-gather.2.cloned.1.call-update
  73.2 0.0 copy-start.1
  73.2 71.8 %all-gather.2.cloned.1.call-done = bf16[768,1,4096]{2,0,1:T(8,128)(2,1)} async-done(((bf16[96,1,4096]{2,0,1:T(8,128)(2,1)}), bf16[768,1,4096]{2,0,1:T(8,128)(2,1)}) %all-gather.2.cloned.1.call-update) | async-done | bytes 6291472 | tf_op jit(solution)/shard_map/all_gather | solution.py:64
  145.0 6.3 %fusion.8 = f32[768,1,192]{0,2,1:T(8,128)} fusion(bf16[1,192,4096]{2,1,0:T(8,128)(2,1)} %param.15, bf16[768,1,4096]{2,0,1:T(8,128)(2,1)} %all-gather.2.cloned.1.call-done), kind=kOutput, calls=%fused_computation.12 | convolution fusion | flops 1207959552 | bytes 8454144 | tf_op jit(solution)/shard_map/red,efd->ref/dot_general | solution.py:65
  151.3 0.0 copy-done
  151.3 0.0 copy-done.1
  151.3 13.0 %fusion.4 = bf16[768,1,4096]{2,0,1:T(8,128)(2,1)} fusion(bf16[1,192,4096]{2,1,0:T(8,128)(2,1)S(1)} %copy-done, bf16[1,192,4096]{2,1,0:T(8,128)(2,1)S(1)} %copy-done.1, bf16[768,1,4096]{2,0,1:T(8,128)(2,1)} %all-gather.2.cloned.1.call-done, f32[768,1,192]{0,2,1:T(8,128)} %fusion.8), kind=kOutput, calls=%fused_computation.6 | convolution fusion | flops 2419949568 | bytes 16318464 | tf_op jit(solution)/shard_map/ref,efd->red/dot_general | solution.py:68
  164.3 10.1 %reshape.122 = bf16[128,6,4096]{2,1,0:T(8,128)(2,1)} reshape(bf16[768,1,4096]{2,0,1:T(8,128)(2,1)} %fusion.4) | data formatting | bytes 12582912 | tf_op jit(solution)/shard_map/reshape | solution.py:69
  174.4 0.0 copy-start.6
  174.4 11.7 %all-to-all-start.1 = ((bf16[128,6,4096]{2,1,0:T(8,128)(2,1)}), bf16[128,6,4096]{2,1,0:T(8,128)(2,1)}, u32[]{:S(2)}, u32[]{:S(2)}) async-start(bf16[128,6,4096]{2,1,0:T(8,128)(2,1)} %reshape.122), calls=%async_computation.2 | async-start | bytes 16777216 | tf_op jit(solution)/shard_map/all_to_all | solution.py:72
  186.1 0.1 reduce_sum.56
  186.2 0.1 mul.72
  186.3 0.0 copy-done.6
  186.3 0.1 convert_reduce_fusion
  186.4 0.1 bitcast_divide_fusion
  186.5 186.5 %all-to-all-done.1 = bf16[128,6,4096]{2,1,0:T(8,128)(2,1)} async-done(((bf16[128,6,4096]{2,1,0:T(8,128)(2,1)}), bf16[128,6,4096]{2,1,0:T(8,128)(2,1)}, u32[]{:S(2)}, u32[]{:S(2)}) %all-to-all-start.1) | async-done | bytes 6291488 | tf_op jit(solution)/shard_map/all_to_all | solution.py:72
  373.0 10.2 %reshape.123 = bf16[8,96,4096]{2,1,0:T(8,128)(2,1)} reshape(bf16[128,6,4096]{2,1,0:T(8,128)(2,1)} %all-to-all-done.1) | data formatting | bytes 12582912 | tf_op jit(solution)/shard_map/reshape | solution.py:75
  383.2 4.0 %reduce_sum.59 = bf16[96,4096]{1,0:T(8,128)(2,1)S(1)} reduce(bf16[8,96,4096]{2,1,0:T(8,128)(2,1)} %reshape.123, bf16[]{:T(256)} %constant.65.clone.1), dimensions={0}, to_apply=%region_6.7 | reduce | flops 2752512 | bytes 7077890 | tf_op jit(solution)/shard_map/reduce_sum | solution.py:76
  387.1 0.0 copy-start.3
  387.2 0.9 gather_fusion
  388.0 0.4 multiply_reduce_fusion
  388.5 0.0 copy-done.3
  388.5 0.7 fusion.43
  (5 shorter events, 0.0 us)
Async XLA Ops:
  6.5 144.8 %copy-start = (bf16[1,192,4096]{2,1,0:T(8,128)(2,1)S(1)}, bf16[1,192,4096]{2,1,0:T(8,128)(2,1)}, u32[]{:S(2)}) copy-start(bf16[1,192,4096]{2,1,0:T(8,128)(2,1)} %param.17) | copy-start | bytes 4718596
  6.5 4.1 %copy-start.4 = (s32[1,8,8]{2,1,0:T(8,128)S(1)}, s32[1,8,8]{2,1,0:T(8,128)}, u32[]{:S(2)}) copy-start(s32[1,8,8]{2,1,0:T(8,128)} %param.13) | copy-start | bytes 772
  6.5 44.3 %copy-start.2 = (bf16[1,8,4096]{2,1,0:T(8,128)(2,1)S(1)}, bf16[1,8,4096]{2,1,0:T(8,128)(2,1)}, u32[]{:S(2)}) copy-start(bf16[1,8,4096]{2,1,0:T(8,128)(2,1)} %param.11) | copy-start | bytes 196612
  6.5 45.3 %copy-start.5 = (f32[4096]{0:T(1024)S(1)}, f32[4096]{0:T(1024)}, u32[]{:S(2)}) copy-start(f32[4096]{0:T(1024)} %param.12) | copy-start | bytes 49156
  6.5 44.3 %reduce-scatter.2.cloned.1.call-start = ((), (), s32[]{:S(2)}) async-start(), calls=%async_computation.3 | async-start | bytes 589824 | tf_op jit(solution)/shard_map/reduce_scatter | solution.py:50
  10.6 134.4 %all-gather.2.cloned.1.call-start = ((), (), s32[]{:S(2)}) async-start(), calls=%async_computation.4 | async-start | bytes 7077888 | tf_op jit(solution)/shard_map/all_gather | solution.py:64
  73.2 78.1 %copy-start.1 = (bf16[1,192,4096]{2,1,0:T(8,128)(2,1)S(1)}, bf16[1,192,4096]{2,1,0:T(8,128)(2,1)}, u32[]{:S(2)}) copy-start(bf16[1,192,4096]{2,1,0:T(8,128)(2,1)} %param.16) | copy-start | bytes 4718596
  174.4 11.9 %copy-start.6 = (s32[1,8,8]{2,1,0:T(8,128)S(1)}, s32[1,8,8]{2,1,0:T(8,128)}, u32[]{:S(2)}) copy-start(s32[1,8,8]{2,1,0:T(8,128)} %param.14) | copy-start | bytes 772
  174.4 198.5 %all-to-all-start.1 = ((bf16[128,6,4096]{2,1,0:T(8,128)(2,1)}), bf16[128,6,4096]{2,1,0:T(8,128)(2,1)}, u32[]{:S(2)}, u32[]{:S(2)}) async-start(bf16[128,6,4096]{2,1,0:T(8,128)(2,1)} %reshape.122), calls=%async_computation.2 | async-start | bytes 16777216 | tf_op jit(solution)/shard_map/all_to_all | solution.py:72
  387.1 1.3 copy-start.3
Sparse Core Ops, SparseCore 0:
  10.7 40.1 reduce-scatter.1
  73.3 71.6 all-gather.1
where the time goes:
time: 397 us; the launch traced here: 396 us
  waiting for transfers between devices  298 us (75%)
  matrix products  24.6 us (6%)
  local copies, waits for them, and re-layouts  24 us (6%)
  blocking collectives  17.6 us (4%)
  between operations  13.5 us (3%)
  starting transfers between devices  11.8 us (3%)
  other arithmetic  6.73 us (2%)
    all_to_all x1, waiting for transfers between devices, on_device(): lax.all_to_all(partial_out, ('tensor', 'expert'), split_axis=0, concat_ax...  186 us
    all_gather x1, waiting for transfers between devices, on_device(): portion = lax.all_gather(arrived, 'tensor', axis=0, tiled=True)  71.8 us
    reduce_scatter x1, waiting for transfers between devices, on_device(): lax.psum_scatter(jnp.dot(head_rows, out_proj, preferred_element_type=jnp....  39.6 us
    all_to_all x1, blocking collectives, on_device(): lax.all_to_all(outgoing, 'expert', split_axis=0, concat_axis=0, tiled=True)  17.6 us
    dot_general x1, matrix products, on_device(): jnp.einsum('ref,efd->red', activated, w_down, preferred_element_type=jnp....  13 us
    all_to_all x1, starting transfers between devices, on_device(): lax.all_to_all(partial_out, ('tensor', 'expert'), split_axis=0, concat_ax...  11.7 us
    reshape x1, local copies, waits for them, and re-layouts, on_device(): received = received.reshape(tensor_count, slot_count, model_width)  10.2 us
    reshape x1, local copies, waits for them, and re-layouts, on_device(): partial_out.astype(jnp.bfloat16)  10.1 us
  transfers between devices with their start and end apart: 3, of which 3 were waited for; matrix products, arithmetic and copies ran while one was open for 0% of the time, Pallas kernels for 0%

commit v1 on v0

--- a/solution.py
+++ b/solution.py
@@ -61,7 +61,9 @@
     )
     arrived = lax.all_to_all(outgoing, "expert", split_axis=0, concat_axis=0, tiled=True)
     arrived = arrived.reshape(expert_count * CAP, per_device, model_width)
-    portion = lax.all_gather(arrived, "tensor", axis=0, tiled=True)
+    portion = jnp.concatenate(
+        lax.all_to_all(jnp.stack([arrived] * lax.axis_size("tensor")), "tensor", 0, 0), axis=0
+    )
     gate_value = jnp.einsum("red,efd->ref", portion, w_gate, preferred_element_type=jnp.float32)
     up_value = jnp.einsum("red,efd->ref", portion, w_up, preferred_element_type=jnp.float32)
     activated = (jax.nn.silu(gate_value) * up_value).astype(jnp.bfloat16)

time: 397 us -> 455 us (1.15)
  blocking collectives: 17.6 us -> 157 us
  waiting for transfers between devices: 298 us -> 219 us
    all_to_all x0 -> x1, blocking collectives: none -> 140 us  [on_device(): lax.all_to_all(jnp.stack([arrived] * lax.axis_size('tensor')), 'tensor',...]
    all_gather x1 -> x0, waiting for transfers between devices: 71.8 us -> none  [on_device(): portion = lax.all_gather(arrived, 'tensor', axis=0, tiled=True)]
    all_to_all x1, waiting for transfers between devices: 186 us -> 180 us  [on_device(): lax.all_to_all(partial_out, ('tensor', 'expert'), split_axis=0, concat_ax...]
  transfers between devices with their start and end apart: 3 -> 2, of which waited for: 3 -> 2; matrix products, arithmetic and copies ran while one was open for 0% -> 0% of each run, Pallas kernels for 0% -> 0%
where the time goes in v1:
time: 455 us; the launch traced here: 454 us
  waiting for transfers between devices  219 us (48%)
  blocking collectives  157 us (35%)
  local copies, waits for them, and re-layouts  26.7 us (6%)
  matrix products  21.2 us (5%)
  between operations  13.5 us (3%)
  starting transfers between devices  9.76 us (2%)
  other arithmetic  6.73 us (1%)
    all_to_all x1, waiting for transfers between devices, on_device(): lax.all_to_all(partial_out, ('tensor', 'expert'), split_axis=0, concat_ax...  180 us
    all_to_all x1, blocking collectives, on_device(): lax.all_to_all(jnp.stack([arrived] * lax.axis_size('tensor')), 'tensor',...  140 us
    reduce_scatter x1, waiting for transfers between devices, on_device(): lax.psum_scatter(jnp.dot(head_rows, out_proj, preferred_element_type=jnp....  39.6 us
    all_to_all x1, blocking collectives, on_device(): lax.all_to_all(outgoing, 'expert', split_axis=0, concat_axis=0, tiled=True)  17.6 us
    dot_general x1, matrix products, on_device(): jnp.einsum('ref,efd->red', activated, w_down, preferred_element_type=jnp....  12.9 us
    reshape x1, local copies, waits for them, and re-layouts, on_device(): received = received.reshape(tensor_count, slot_count, model_width)  10.2 us
    reshape x1, local copies, waits for them, and re-layouts, on_device(): partial_out.astype(jnp.bfloat16)  10.1 us
    all_to_all x1, starting transfers between devices, on_device(): lax.all_to_all(partial_out, ('tensor', 'expert'), split_axis=0, concat_ax...  9.73 us
  transfers between devices with their start and end apart: 2, of which 2 were waited for; matrix products, arithmetic and copies ran while one was open for 0% of the time, Pallas kernels for 0%

profile of v1, /device:TPU:6, one launch (start us, length us, event | category | flops | bytes accessed | tf_op | source)
XLA Modules:
  0.0 454.2 jit_solution(1593618753686704789)
XLA Ops:
  6.5 0.0 copy-start
  6.5 0.0 copy-start.5
  6.5 0.0 copy-start.3
  6.5 0.0 copy-start.6
  6.5 0.0 reduce-scatter.2.cloned.1.call-start
  6.6 4.0 convolution_convert_fusion.2
  10.6 0.0 reduce-scatter.2.cloned.1.call-update
  10.6 0.0 copy-done.5
  10.6 0.1 reshape_squeeze.3
  10.7 0.1 fusion.29
  10.7 0.1 reduce_window_sum.11
  10.8 0.2 select_reduce_fusion
  11.0 0.1 reduce_sum.57
  11.1 0.1 fusion.30
  11.2 39.6 %reduce-scatter.2.cloned.1.call-done = bf16[8,4096]{1,0:T(8,128)(2,1)} async-done(((bf16[64,4096]{1,0:T(8,128)(2,1)}), bf16[8,4096]{1,0:T(8,128)(2,1)}) %reduce-scatter.2.cloned.1.call-update) | async-done | bytes 65552 | tf_op jit(solution)/shard_map/reduce_scatter | solution.py:50
  50.9 0.0 copy-done.3
  50.9 1.0 multiply_reduce_fusion.1
  51.8 0.0 copy-done.6
  51.9 1.3 convolution_convert_fusion.1
  53.1 0.3 reshape.119
  53.4 17.6 %all_to_all.15 = bf16[16,6,4096]{2,1,0:T(8,128)(2,1)} all-to-all(bf16[16,6,4096]{2,1,0:T(8,128)(2,1)S(1)} %reshape.119), channel_id=1, replica_groups=mesh['dp'=2,'tensor'=8,'expert'=16] {'expert'}, dimensions={0} | all-to-all | bytes 1572864 | tf_op jit(solution)/shard_map/all_to_all | solution.py:62
  71.0 1.4 stack_reshape.2
  72.4 0.8 stack.3
  73.2 0.0 copy-start.8
  73.2 139.6 %all_to_all.16 = bf16[8,96,1,4096]{3,1,2,0:T(8,128)(2,1)S(1)} all-to-all(bf16[8,96,1,4096]{3,1,2,0:T(8,128)(2,1)S(1)} %stack.3), channel_id=1, replica_groups=mesh['dp'=2,'tensor'=8,'expert'=16] {'tensor'}, dimensions={0} | all-to-all | bytes 12582912 | tf_op jit(solution)/shard_map/all_to_all | solution.py:65
  212.8 0.0 copy-start.1
  212.8 2.7 copy-done.1
  215.4 0.0 copy-done.8
  215.4 0.0 copy-start.2
  215.4 3.1 fusion.6
  218.5 0.0 copy-done
  218.5 0.0 copy-done.2
  218.5 12.9 %fusion = bf16[768,1,4096]{2,0,1:T(8,128)(2,1)} fusion(bf16[1,192,4096]{2,1,0:T(8,128)(2,1)S(1)} %copy-done, bf16[768,4096]{1,0:T(8,128)(2,1)} %bitcast.92, bf16[1,192,4096]{2,1,0:T(8,128)(2,1)S(1)} %copy-done.2, f32[768,1,192]{0,2,1:T(8,128)} %fusion.6), kind=kOutput, calls=%fused_computation.2 | convolution fusion | flops 2419949568 | bytes 16318464 | tf_op jit(solution)/shard_map/ref,efd->red/dot_general | solution.py:70
  231.4 10.1 %reshape.125 = bf16[128,6,4096]{2,1,0:T(8,128)(2,1)} reshape(bf16[768,1,4096]{2,0,1:T(8,128)(2,1)} %fusion) | data formatting | bytes 12582912 | tf_op jit(solution)/shard_map/reshape | solution.py:71
  241.5 0.0 copy-start.7
  241.5 9.7 %all-to-all-start.2 = ((bf16[128,6,4096]{2,1,0:T(8,128)(2,1)}), bf16[128,6,4096]{2,1,0:T(8,128)(2,1)}, u32[]{:S(2)}, u32[]{:S(2)}) async-start(bf16[128,6,4096]{2,1,0:T(8,128)(2,1)} %reshape.125), calls=%async_computation.3 | async-start | bytes 16777216 | tf_op jit(solution)/shard_map/all_to_all | solution.py:74
  251.3 0.1 reduce_sum.56
  251.4 0.1 mul.72
  251.5 0.0 copy-done.7
  251.5 0.1 convert_reduce_fusion
  251.6 0.1 bitcast_divide_fusion
  251.7 179.5 %all-to-all-done.2 = bf16[128,6,4096]{2,1,0:T(8,128)(2,1)} async-done(((bf16[128,6,4096]{2,1,0:T(8,128)(2,1)}), bf16[128,6,4096]{2,1,0:T(8,128)(2,1)}, u32[]{:S(2)}, u32[]{:S(2)}) %all-to-all-start.2) | async-done | bytes 6291488 | tf_op jit(solution)/shard_map/all_to_all | solution.py:74
  431.2 10.2 %reshape.126 = bf16[8,96,4096]{2,1,0:T(8,128)(2,1)} reshape(bf16[128,6,4096]{2,1,0:T(8,128)(2,1)} %all-to-all-done.2) | data formatting | bytes 12582912 | tf_op jit(solution)/shard_map/reshape | solution.py:77
  441.4 4.0 reduce_sum.59
  445.4 0.0 copy-start.4
  445.4 0.9 gather_fusion
  446.3 0.4 multiply_reduce_fusion
  446.7 0.0 copy-done.4
  446.7 0.7 fusion.24
  (5 shorter events, 0.0 us)
Async XLA Ops:
  6.5 212.0 %copy-start = (bf16[1,192,4096]{2,1,0:T(8,128)(2,1)S(1)}, bf16[1,192,4096]{2,1,0:T(8,128)(2,1)}, u32[]{:S(2)}) copy-start(bf16[1,192,4096]{2,1,0:T(8,128)(2,1)} %param.17) | copy-start | bytes 4718596
  6.5 4.0 copy-start.5
  6.5 44.3 %copy-start.3 = (bf16[1,8,4096]{2,1,0:T(8,128)(2,1)S(1)}, bf16[1,8,4096]{2,1,0:T(8,128)(2,1)}, u32[]{:S(2)}) copy-start(bf16[1,8,4096]{2,1,0:T(8,128)(2,1)} %param.11) | copy-start | bytes 196612
  6.5 45.3 %copy-start.6 = (f32[4096]{0:T(1024)S(1)}, f32[4096]{0:T(1024)}, u32[]{:S(2)}) copy-start(f32[4096]{0:T(1024)} %param.12) | copy-start | bytes 49156
  6.5 44.3 %reduce-scatter.2.cloned.1.call-start = ((), (), s32[]{:S(2)}) async-start(), calls=%async_computation.4 | async-start | bytes 589824 | tf_op jit(solution)/shard_map/reduce_scatter | solution.py:50
  73.2 142.2 %copy-start.8 = (bf16[1,192,4096]{2,1,0:T(8,128)(2,1)S(1)}, bf16[1,192,4096]{2,1,0:T(8,128)(2,1)}, u32[]{:S(2)}) copy-start(bf16[1,192,4096]{2,1,0:T(8,128)(2,1)} %param.15) | copy-start | bytes 4718596
  212.8 2.7 copy-start.1
  215.4 3.1 copy-start.2
  241.5 9.9 %copy-start.7 = (s32[1,8,8]{2,1,0:T(8,128)S(1)}, s32[1,8,8]{2,1,0:T(8,128)}, u32[]{:S(2)}) copy-start(s32[1,8,8]{2,1,0:T(8,128)} %param.14) | copy-start | bytes 772
  241.5 189.7 %all-to-all-start.2 = ((bf16[128,6,4096]{2,1,0:T(8,128)(2,1)}), bf16[128,6,4096]{2,1,0:T(8,128)(2,1)}, u32[]{:S(2)}, u32[]{:S(2)}) async-start(bf16[128,6,4096]{2,1,0:T(8,128)(2,1)} %reshape.125), calls=%async_computation.3 | async-start | bytes 16777216 | tf_op jit(solution)/shard_map/all_to_all | solution.py:74
  445.4 1.3 copy-start.4
Sparse Core Ops, SparseCore 0:
  10.7 40.1 reduce-scatter.1
